TPU v7x, 32 devices: a whole 2x2x4 slice. The times are simulated.
32 devices in a mesh: dp: 8 (over z, y), space: 4 (over x, core).
Axes of the slice: x: 2, y: 2, z: 4, core: 2. Of those that a mesh axis runs over, the one named last changes fastest.
Arguments:
- volume: bfloat16 [8, 4, 32, 32, 32], P('dp', None, 'space'), may hold values from -6 to 6
- cotangent: bfloat16 [8, 64, 512], P('dp', None, 'space'), may hold values from -6 to 6
- conv_one: bfloat16 [32, 4, 3, 3, 3], replicated, may hold values from -0.625 to 0.625
- conv_two: bfloat16 [64, 32, 3, 3, 3], replicated, may hold values from -0.21875 to 0.21875
Outputs:
- out_two: bfloat16 [8, 64, 512], P('dp', None, 'space')
- grad_pre: bfloat16 [8, 32, 4096], P('dp', None, 'space')
- update_one: float32 [3456], replicated
- update_two: float32 [55296], replicated
All inputs are finite; a program needn't handle non-finite values.
Results may differ from a plain program's by a relative error of at most 0.0057.
Values may be sent and summed in bfloat16 or wider, within the bound.
A program may use at most 64 MiB of HBM per device.

v0:
```python
import jax
import jax.numpy as jnp
from jax import lax
from jax.sharding import PartitionSpec as P

damp_input = 0.1
damp_grad = 0.03


def passed_along(value, axis, steps):
    count = lax.axis_size(axis)
    leading, last = (max(0, -steps), min(count, count - steps))
    return lax.ppermute(value, axis, [(source, source + steps) for source in range(leading, last)])


def tap_stack(padded, out_depth, out_rows, out_cols):
    pieces = []
    for depth_tap in range(3):
        for row_tap in range(3):
            for col_tap in range(3):
                pieces.append(
                    padded[
                        :,
                        depth_tap : depth_tap + 2 * out_depth : 2,
                        row_tap : row_tap + 2 * out_rows : 2,
                        col_tap : col_tap + 2 * out_cols : 2,
                    ]
                )
    stacked = jnp.stack(pieces, axis=1)
    return stacked.reshape(stacked.shape[0] * 27, -1)


def spread_taps(columns, channels, out_depth, out_rows, out_cols):
    pieces = columns.reshape(channels, 27, out_depth, out_rows, out_cols)
    canvas = jnp.zeros(
        (channels, 2 * out_depth + 1, 2 * out_rows + 1, 2 * out_cols + 1), jnp.float32
    )
    for depth_tap in range(3):
        for row_tap in range(3):
            for col_tap in range(3):
                tap_number = depth_tap * 9 + row_tap * 3 + col_tap
                canvas = canvas.at[
                    :,
                    depth_tap : depth_tap + 2 * out_depth : 2,
                    row_tap : row_tap + 2 * out_rows : 2,
                    col_tap : col_tap + 2 * out_cols : 2,
                ].add(pieces[:, tap_number])
    return canvas


def silu_slope(pre_act):
    sigmoid_val = jax.nn.sigmoid(pre_act)
    return sigmoid_val * (1.0 + pre_act * (1.0 - sigmoid_val))


def damped_solve(matrix, rhs_terms):
    lower_factor = jnp.linalg.cholesky(matrix)
    return jax.scipy.linalg.cho_solve((lower_factor, True), rhs_terms)


def precondition(gram_in, gram_out, grad_sum, total_rows):
    in_mat = gram_in / total_rows + damp_input * jnp.eye(gram_in.shape[0], dtype=jnp.float32)
    out_mat = gram_out / total_rows + damp_grad * jnp.eye(gram_out.shape[0], dtype=jnp.float32)
    mean_grad = grad_sum / total_rows
    half_solved = damped_solve(in_mat, mean_grad.T).T
    return (damped_solve(out_mat, half_solved), mean_grad)


def on_device(volume, cotangent, conv_one, conv_two):
    local_volume = volume[0]
    cot_flat = cotangent[0]
    depth_len, row_count, col_count = (
        local_volume.shape[1],
        local_volume.shape[2],
        local_volume.shape[3],
    )
    width_one = conv_one.shape[0]
    width_two = conv_two.shape[0]
    weight_one = conv_one.reshape(width_one, -1)
    weight_two = conv_two.reshape(width_two, -1)
    lower_plane = passed_along(local_volume[:, depth_len - 1], "space", 1)
    extended = jnp.concatenate([lower_plane[:, None], local_volume], axis=1)
    padded = jnp.pad(extended, ((0, 0), (0, 0), (1, 0), (1, 0)))
    first_cols = tap_stack(padded, depth_len // 2, row_count // 2, col_count // 2)
    pre_one = jnp.dot(weight_one, first_cols, preferred_element_type=jnp.float32)
    act_one = (
        jax.nn.silu(pre_one)
        .astype(jnp.bfloat16)
        .reshape(width_one, depth_len // 2, row_count // 2, col_count // 2)
    )
    lower_act = passed_along(act_one[:, depth_len // 2 - 1], "space", 1)
    extended_two = jnp.concatenate([lower_act[:, None], act_one], axis=1)
    padded_two = jnp.pad(extended_two, ((0, 0), (0, 0), (1, 0), (1, 0)))
    second_cols = tap_stack(padded_two, depth_len // 4, row_count // 4, col_count // 4)
    out_two = jnp.dot(weight_two, second_cols, preferred_element_type=jnp.float32).astype(
        jnp.bfloat16
    )
    back_cols = jnp.dot(weight_two.T, cot_flat, preferred_element_type=jnp.float32)
    canvas = spread_taps(back_cols, width_one, depth_len // 4, row_count // 4, col_count // 4)
    grad_act = canvas[:, 1:, 1:, 1:]
    upper_part = passed_along(canvas[:, 0, 1:, 1:].astype(jnp.bfloat16), "space", -1).astype(
        jnp.float32
    )
    grad_act = grad_act.at[:, -1].add(upper_part)
    grad_pre = (grad_act.reshape(width_one, -1) * silu_slope(pre_one)).astype(jnp.bfloat16)
    in_one = jnp.dot(first_cols, first_cols.T, preferred_element_type=jnp.float32)
    gram_one = jnp.dot(grad_pre, grad_pre.T, preferred_element_type=jnp.float32)
    grad_one = jnp.dot(grad_pre, first_cols.T, preferred_element_type=jnp.float32)
    in_two = jnp.dot(second_cols, second_cols.T, preferred_element_type=jnp.float32)
    gram_two = jnp.dot(cot_flat, cot_flat.T, preferred_element_type=jnp.float32)
    grad_two = jnp.dot(cot_flat, second_cols.T, preferred_element_type=jnp.float32)
    summed = lax.psum((in_two, in_one, gram_one, grad_one, gram_two, grad_two), ("dp", "space"))
    total_in_two, total_in_one, total_gram_one, total_grad_one, total_gram_two, total_grad_two = (
        summed
    )
    device_count = lax.axis_size("dp") * lax.axis_size("space")
    rows_one = first_cols.shape[1] * device_count
    rows_two = cot_flat.shape[1] * device_count
    step_one, mean_one = precondition(total_in_one, total_gram_one, total_grad_one, rows_one)
    step_two, mean_two = precondition(total_in_two, total_gram_two, total_grad_two, rows_two)
    quad_form = jnp.sum(step_one * mean_one) + jnp.sum(step_two * mean_two)
    factor = jnp.sqrt((step_one.size + step_two.size) / quad_form)
    update_one = (factor * step_one).reshape(-1)
    update_two = (factor * step_two).reshape(-1)
    return (out_two[None], grad_pre[None], update_one, update_two)


def solution(mesh):
    in_specs = (P("dp", None, "space", None, None), P("dp", None, "space"), P(), P())
    out_specs = (P("dp", None, "space"), P("dp", None, "space"), P(), P())
    return jax.shard_map(
        on_device, mesh=mesh, in_specs=in_specs, out_specs=out_specs, check_vma=False
    )
```

profile of v0, /device:TPU:0, one launch (start us, length us, event | category | flops | bytes accessed | tf_op | source)
XLA Modules:
  0.0 933.9 jit_solution(1185647925688393770)
XLA Ops:
  21.5 8.7 scatter_fusion.1
  38.9 8.7 scatter_fusion.3
  65.0 8.7 scatter_fusion.6
  73.7 8.7 scatter_fusion.7
  117.1 8.9 scatter_fusion.12
  221.7 9.1 scatter_fusion.24
  390.8 104.5 %all-reduce.10.cloned.1.call-done = (f32[108,108]{1,0:T(8,128)}, f32[32,108]{1,0:T(8,128)}, f32[32,32]{1,0:T(8,128)}, f32[64,64]{1,0:T(8,128)}) async-done(((f32[108,108]{1,0:T(8,128)}, f32[32,108]{1,0:T(8,128)}, f32[32,32]{1,0:T(8,128)}, f32[64,64]{1,0:T(8,128)}), (f32[108,108]{1,0:T(8,128)}, f32[32,108]{1,0:T(8,128)}, f32[32,32]{1,0:T(8,128)}, f32[64,64]{1,0:T(8,128)})) %all-reduce.10.cloned.1.call-update) | async-done | bytes 80976 | tf_op jit(solution)/shard_map/psum | solution.py:112
  497.0 9.9 %cholesky.246 = f32[108,108]{1,0:T(8,128)S(1)} custom-call(f32[108,108]{1,0:T(8,128)S(1)} %fusion.98), custom_call_target="Cholesky" | custom-call | tf_op jit(solution)/shard_map/jit(cholesky)/cholesky | solution.py:57
  542.7 97.4 %all-reduce.12.cloned.1.call-done = (f32[864,864]{1,0:T(8,128)}, f32[64,864]{1,0:T(8,128)}) async-done(((f32[864,864]{1,0:T(8,128)}, f32[64,864]{1,0:T(8,128)}), (f32[864,864]{1,0:T(8,128)}, f32[64,864]{1,0:T(8,128)})) %all-reduce.12.cloned.1.call-update) | async-done | bytes 3207184 | tf_op jit(solution)/shard_map/psum | solution.py:112
  652.4 11.7 %cholesky.269 = f32[128,128]{1,0:T(8,128)S(1)} custom-call(f32[128,128]{1,0:T(8,128)S(1)} %cholesky.607), custom_call_target="Cholesky" | custom-call | tf_op jit(solution)/shard_map/jit(cholesky)/cholesky | solution.py:57
  665.1 9.8 %custom-call.91 = f32[1,128,128]{1,2,0:T(8,128)S(1)} custom-call(f32[1,128,128]{2,1,0:T(8,128)S(1)} %get-tuple-element.85), custom_call_target="InvertDiagBlocksLowerTriangular" | custom-call | tf_op jit(solution)/shard_map/jit(cholesky)/cholesky | solution.py:57
  678.4 12.5 %cholesky.492 = f32[128,128]{1,0:T(8,128)S(1)} custom-call(f32[128,128]{1,0:T(8,128)} %cholesky.611), custom_call_target="Cholesky" | custom-call | tf_op jit(solution)/shard_map/jit(cholesky)/cholesky | solution.py:57
  691.6 11.0 %custom-call.92 = f32[1,128,128]{1,2,0:T(8,128)S(1)} custom-call(f32[1,128,128]{2,1,0:T(8,128)} %get-tuple-element.82), custom_call_target="InvertDiagBlocksLowerTriangular" | custom-call | tf_op jit(solution)/shard_map/jit(cholesky)/cholesky | solution.py:57
  704.7 11.7 %cholesky.513 = f32[128,128]{1,0:T(8,128)S(1)} custom-call(f32[128,128]{1,0:T(8,128)S(1)} %cholesky.616), custom_call_target="Cholesky" | custom-call | tf_op jit(solution)/shard_map/jit(cholesky)/cholesky | solution.py:57
  716.5 9.8 %custom-call.93 = f32[1,128,128]{1,2,0:T(8,128)S(1)} custom-call(f32[1,128,128]{2,1,0:T(8,128)S(1)} %get-tuple-element.79), custom_call_target="InvertDiagBlocksLowerTriangular" | custom-call | tf_op jit(solution)/shard_map/jit(cholesky)/cholesky | solution.py:57
  728.3 11.9 %cholesky.532 = f32[128,128]{1,0:T(8,128)S(1)} custom-call(f32[128,128]{1,0:T(8,128)S(1)} %cholesky.621), custom_call_target="Cholesky" | custom-call | tf_op jit(solution)/shard_map/jit(cholesky)/cholesky | solution.py:57
  740.2 9.8 %custom-call.94 = f32[1,128,128]{1,2,0:T(8,128)S(1)} custom-call(f32[1,128,128]{2,1,0:T(8,128)S(1)} %get-tuple-element.76), custom_call_target="InvertDiagBlocksLowerTriangular" | custom-call | tf_op jit(solution)/shard_map/jit(cholesky)/cholesky | solution.py:57
  752.0 11.7 %cholesky.551 = f32[128,128]{1,0:T(8,128)S(1)} custom-call(f32[128,128]{1,0:T(8,128)S(1)} %cholesky.626), custom_call_target="Cholesky" | custom-call | tf_op jit(solution)/shard_map/jit(cholesky)/cholesky | solution.py:57
  763.8 9.8 %custom-call.95 = f32[1,128,128]{1,2,0:T(8,128)S(1)} custom-call(f32[1,128,128]{2,1,0:T(8,128)S(1)} %get-tuple-element.73), custom_call_target="InvertDiagBlocksLowerTriangular" | custom-call | tf_op jit(solution)/shard_map/jit(cholesky)/cholesky | solution.py:57
  775.4 11.9 %cholesky.571 = f32[128,128]{1,0:T(8,128)S(1)} custom-call(f32[128,128]{1,0:T(8,128)S(1)} %cholesky.631), custom_call_target="Cholesky" | custom-call | tf_op jit(solution)/shard_map/jit(cholesky)/cholesky | solution.py:57
  787.4 9.8 %custom-call.96 = f32[1,128,128]{1,2,0:T(8,128)S(1)} custom-call(f32[1,128,128]{2,1,0:T(8,128)S(1)} %get-tuple-element.70), custom_call_target="InvertDiagBlocksLowerTriangular" | custom-call | tf_op jit(solution)/shard_map/jit(cholesky)/cholesky | solution.py:57
  798.6 8.8 cholesky.592
  818.4 18.1 %while.2 = (s32[]{:T(128)}, f32[864,864]{1,0:T(8,128)}, s32[6,2]{0,1:T(2,128)S(1)}, f32[6,128,128]{2,1,0:T(8,128)S(1)}, s32[]{:T(128)}) while((s32[]{:T(128)}, f32[864,864]{1,0:T(8,128)}, s32[6,2]{0,1:T(2,128)S(1)}, f32[6,128,128]{2,1,0:T(8,128)S(1)}, s32[]{:T(128)}) %tuple.123), condition=%wide.while_cond.1, body=%wide.while_body.1.sunk | while | flops 2 | bytes 131189 | solution.py:58
  838.4 69.8 %custom-call.97 = f32[7,128,128]{1,2,0:T(8,128)S(1)} custom-call(f32[7,128,128]{2,1,0:T(8,128)} %pad_maximum_fusion), custom_call_target="InvertDiagBlocksLowerTriangular" | custom-call | tf_op jit(solution)/shard_map/jit(_cho_solve)/triangular_solve | solution.py:58
  (374 shorter events, 437.0 us)
Async XLA Ops:
  7.2 488.1 %all-reduce.10.cloned.1.call-start = ((), (), s32[]{:S(2)}) async-start(), calls=%async_computation | async-start | bytes 245760 | tf_op jit(solution)/shard_map/psum | solution.py:112
  239.5 10.6 %copy-start.8 = (bf16[1,4,8,32,32]{4,3,2,1,0:T(8,128)(2,1)S(1)}, bf16[1,4,8,32,32]{4,3,2,1,0:T(8,128)(2,1)}, u32[]{:S(2)}) copy-start(bf16[1,4,8,32,32]{4,3,2,1,0:T(8,128)(2,1)} %param.6) | copy-start | bytes 196612
  239.5 13.7 %copy-start.10 = (bf16[1,64,128]{2,1,0:T(8,128)(2,1)S(1)}, bf16[1,64,128]{2,1,0:T(8,128)(2,1)}, u32[]{:S(2)}) copy-start(bf16[1,64,128]{2,1,0:T(8,128)(2,1)} %param.7) | copy-start | bytes 49156
  239.5 15.7 %copy-start.12 = (bf16[32,4,3,3,3]{0,1,4,3,2:T(4,128)(2,1)S(1)}, bf16[32,4,3,3,3]{0,1,4,3,2:T(4,128)(2,1)}, u32[]{:S(2)}) copy-start(bf16[32,4,3,3,3]{0,1,4,3,2:T(4,128)(2,1)} %param.8) | copy-start | bytes 20740
  248.8 112.8 %collective-permute-start.2 = (bf16[32,16,16]{0,2,1:T(8,128)(2,1)}, bf16[32,16,16]{0,2,1:T(8,128)(2,1)}, u32[]{:S(2)}, u32[]{:S(2)}) collective-permute-start(bf16[32,16,16]{0,2,1:T(8,128)(2,1)} %fusion.66), channel_id=1, source_target_pairs={{1,0},{2,1},{3,2},{5,4},{6,5},{7,6},{9,8},{10,9},{11,10},{13,12},{... | collective-permute-start | bytes 49160 | tf_op jit(solution)/shard_map/ppermute | solution.py:13
  250.2 5.1 collective-permute-start
  362.8 20.5 %copy-start.4 = (bf16[32,1024]{1,0:T(8,128)(2,1)}, bf16[32,1024]{1,0:T(8,128)(2,1)S(1)}, u32[]{:S(2)}) copy-start(bf16[32,1024]{1,0:T(8,128)(2,1)S(1)} %get-tuple-element.67) | copy-start | bytes 196612
  363.0 6.1 collective-permute-start.1
  369.0 271.0 %all-reduce.12.cloned.1.call-start = ((), (), s32[]{:S(2)}) async-start(), calls=%async_computation.1 | async-start | bytes 6651904 | tf_op jit(solution)/shard_map/psum | solution.py:112
  643.9 4.6 copy-start
  650.8 1.6 copy-start.3
  652.4 12.0 %copy-start.5 = (f32[64,864]{1,0:T(8,128)S(1)}, f32[64,864]{1,0:T(8,128)}, u32[]{:S(2)}) copy-start(f32[64,864]{1,0:T(8,128)} %get-tuple-element.37) | copy-start | bytes 663556
  816.4 0.9 copy-start.13
  816.4 1.9 copy-start.7
  816.5 20.1 %copy-start.9 = (f32[128,32]{1,0:T(8,128)S(1)}, f32[128,32]{1,0:T(8,128)}, u32[]{:S(2)}) copy-start(f32[128,32]{1,0:T(8,128)} %pad_convert_fusion) | copy-start | bytes 49156
  816.7 1.7 copy-start.1
  836.5 78.4 %copy-start.2 = (f32[864,864]{1,0:T(8,128)S(1)}, f32[864,864]{1,0:T(8,128)}, u32[]{:S(2)}) copy-start(f32[864,864]{1,0:T(8,128)} %get-tuple-element.214) | copy-start | bytes 8957956
  913.3 8.2 copy-start.11
  914.9 7.1 copy-start.6
Sparse Core Ops, SparseCore 0:
  369.2 126.0 all-reduce.9
  500.9 139.1 all-reduce.11
where the time goes:
time: 946 us; the launch traced here: 934 us
  other arithmetic  507 us (54%)
  waiting for transfers between devices  202 us (21%)
  local copies, waits for them, and re-layouts  157 us (17%)
  matrix products  37.8 us (4%)
  between operations  22.1 us (2%)
    scatter-add x27, other arithmetic, spread_taps(): canvas = canvas.at[:, depth_tap:depth_tap + 2 * out_depth:2, row_tap:row_...  235 us
    psum x2, waiting for transfers between devices, on_device(): lax.psum((in_two, in_one, gram_one, grad_one, gram_two, grad_two), ('dp',...  202 us
    another operation x36, other arithmetic, damped_solve(): lower_factor = jnp.linalg.cholesky(matrix)  166 us
    another operation x13, other arithmetic, damped_solve(): return jax.scipy.linalg.cho_solve((lower_factor, True), rhs_terms)  91.3 us
    slice x54, local copies, waits for them, and re-layouts, tap_stack(): padded[:, depth_tap:depth_tap + 2 * out_depth:2, row_tap:row_tap + 2 * ou...  90.9 us
    unnamed x95, local copies, waits for them, and re-layouts  27 us
  transfers between devices with their start and end apart: 5, of which 2 were waited for; matrix products, arithmetic and copies ran while one was open for 19% of the time, Pallas kernels for 0%

commit v1 on v0

--- a/solution.py
+++ b/solution.py
@@ -109,7 +109,9 @@
     in_two = jnp.dot(second_cols, second_cols.T, preferred_element_type=jnp.float32)
     gram_two = jnp.dot(cot_flat, cot_flat.T, preferred_element_type=jnp.float32)
     grad_two = jnp.dot(cot_flat, second_cols.T, preferred_element_type=jnp.float32)
-    summed = lax.psum((in_two, in_one, gram_one, grad_one, gram_two, grad_two), ("dp", "space"))
+    summed = (in_two, in_one, gram_one, grad_one, gram_two, grad_two)
+    for over in ("space", "dp"):
+        summed = lax.psum(summed, over)
     total_in_two, total_in_one, total_gram_one, total_grad_one, total_gram_two, total_grad_two = (
         summed
     )

time: 946 us -> 999 us (1.056)
  waiting for transfers between devices: 202 us -> 255 us
    psum x2 -> x4, waiting for transfers between devices: 202 us -> 255 us  [on_device(): summed = lax.psum(summed, over)]
    unnamed x95 -> x101, local copies, waits for them, and re-layouts: 27 us -> 27.1 us
  transfers between devices with their start and end apart: 5 -> 7, of which waited for: 2 -> 4; matrix products, arithmetic and copies ran while one was open for 19% -> 17% of each run, Pallas kernels for 0% -> 0%
where the time goes in v1:
time: 999 us; the launch traced here: 987 us
  other arithmetic  507 us (51%)
  waiting for transfers between devices  255 us (26%)
  local copies, waits for them, and re-layouts  157 us (16%)
  matrix products  37.2 us (4%)
  between operations  21.6 us (2%)
    psum x4, waiting for transfers between devices, on_device(): summed = lax.psum(summed, over)  255 us
    scatter-add x27, other arithmetic, spread_taps(): canvas = canvas.at[:, depth_tap:depth_tap + 2 * out_depth:2, row_tap:row_...  235 us
    another operation x36, other arithmetic, damped_solve(): lower_factor = jnp.linalg.cholesky(matrix)  171 us
    slice x54, local copies, waits for them, and re-layouts, tap_stack(): padded[:, depth_tap:depth_tap + 2 * out_depth:2, row_tap:row_tap + 2 * ou...  91 us
    another operation x13, other arithmetic, damped_solve(): return jax.scipy.linalg.cho_solve((lower_factor, True), rhs_terms)  90.6 us
    unnamed x101, local copies, waits for them, and re-layouts  27.1 us
  transfers between devices with their start and end apart: 7, of which 4 were waited for; matrix products, arithmetic and copies ran while one was open for 17% of the time, Pallas kernels for 0%

profile of v1, /device:TPU:0, one launch (start us, length us, event | category | flops | bytes accessed | tf_op | source)
XLA Modules:
  0.0 987.1 jit_solution(9919888693411945717)
XLA Ops:
  12.8 8.7 scatter_fusion
  38.9 8.7 scatter_fusion.3
  117.1 9.2 scatter_fusion.12
  221.9 8.9 scatter_fusion.24
  387.8 13.8 %all-reduce.18.cloned.1.call-done = (f32[108,108]{1,0:T(8,128)}, f32[32,108]{1,0:T(8,128)}, f32[32,32]{1,0:T(8,128)}, f32[64,64]{1,0:T(8,128)}) async-done(((f32[108,108]{1,0:T(8,128)}, f32[32,108]{1,0:T(8,128)}, f32[32,32]{1,0:T(8,128)}, f32[64,64]{1,0:T(8,128)}), (f32[108,108]{1,0:T(8,128)}, f32[32,108]{1,0:T(8,128)}, f32[32,32]{1,0:T(8,128)}, f32[64,64]{1,0:T(8,128)})) %all-reduce.18.cloned.1.call-update) | async-done | bytes 80976 | tf_op jit(solution)/shard_map/psum | solution.py:114
  404.2 72.0 %all-reduce.14.cloned.1.call-done = (f32[108,108]{1,0:T(8,128)}, f32[32,108]{1,0:T(8,128)}, f32[32,32]{1,0:T(8,128)}, f32[64,64]{1,0:T(8,128)}) async-done(((f32[108,108]{1,0:T(8,128)}, f32[32,108]{1,0:T(8,128)}, f32[32,32]{1,0:T(8,128)}, f32[64,64]{1,0:T(8,128)}), (f32[108,108]{1,0:T(8,128)}, f32[32,108]{1,0:T(8,128)}, f32[32,32]{1,0:T(8,128)}, f32[64,64]{1,0:T(8,128)})) %all-reduce.14.cloned.1.call-update) | async-done | bytes 80976 | tf_op jit(solution)/shard_map/psum | solution.py:114
  477.3 73.0 %all-reduce.20.cloned.1.call-done = (f32[864,864]{1,0:T(8,128)}, f32[64,864]{1,0:T(8,128)}) async-done(((f32[864,864]{1,0:T(8,128)}, f32[64,864]{1,0:T(8,128)}), (f32[864,864]{1,0:T(8,128)}, f32[64,864]{1,0:T(8,128)})) %all-reduce.20.cloned.1.call-update) | async-done | bytes 3207184 | tf_op jit(solution)/shard_map/psum | solution.py:114
  550.3 9.9 %cholesky.246 = f32[108,108]{1,0:T(8,128)S(1)} custom-call(f32[108,108]{1,0:T(8,128)S(1)} %fusion.98), custom_call_target="Cholesky" | custom-call | tf_op jit(solution)/shard_map/jit(cholesky)/cholesky | solution.py:57
  591.6 96.1 %all-reduce.16.cloned.1.call-done = (f32[864,864]{1,0:T(8,128)}, f32[64,864]{1,0:T(8,128)}) async-done(((f32[864,864]{1,0:T(8,128)}, f32[64,864]{1,0:T(8,128)}), (f32[864,864]{1,0:T(8,128)}, f32[64,864]{1,0:T(8,128)})) %all-reduce.16.cloned.1.call-update) | async-done | bytes 3207184 | tf_op jit(solution)/shard_map/psum | solution.py:114
  700.3 11.7 %cholesky.269 = f32[128,128]{1,0:T(8,128)S(1)} custom-call(f32[128,128]{1,0:T(8,128)S(1)} %cholesky.607), custom_call_target="Cholesky" | custom-call | tf_op jit(solution)/shard_map/jit(cholesky)/cholesky | solution.py:57
  712.9 9.8 custom-call.91
  726.3 13.2 %cholesky.492 = f32[128,128]{1,0:T(8,128)} custom-call(f32[128,128]{1,0:T(8,128)} %cholesky.611), custom_call_target="Cholesky" | custom-call | tf_op jit(solution)/shard_map/jit(cholesky)/cholesky | solution.py:57
  741.0 11.4 %custom-call.92 = f32[1,128,128]{1,2,0:T(8,128)} custom-call(f32[1,128,128]{2,1,0:T(8,128)} %get-tuple-element.88), custom_call_target="InvertDiagBlocksLowerTriangular" | custom-call | tf_op jit(solution)/shard_map/jit(cholesky)/cholesky | solution.py:57
  755.9 12.5 %cholesky.513 = f32[128,128]{1,0:T(8,128)S(1)} custom-call(f32[128,128]{1,0:T(8,128)} %cholesky.616), custom_call_target="Cholesky" | custom-call | tf_op jit(solution)/shard_map/jit(cholesky)/cholesky | solution.py:57
  769.1 10.6 %custom-call.93 = f32[1,128,128]{1,2,0:T(8,128)S(1)} custom-call(f32[1,128,128]{2,1,0:T(8,128)} %get-tuple-element.85), custom_call_target="InvertDiagBlocksLowerTriangular" | custom-call | tf_op jit(solution)/shard_map/jit(cholesky)/cholesky | solution.py:57
  781.8 11.9 %cholesky.532 = f32[128,128]{1,0:T(8,128)S(1)} custom-call(f32[128,128]{1,0:T(8,128)S(1)} %cholesky.621), custom_call_target="Cholesky" | custom-call | tf_op jit(solution)/shard_map/jit(cholesky)/cholesky | solution.py:57
  793.7 9.8 custom-call.94
  805.5 11.7 %cholesky.551 = f32[128,128]{1,0:T(8,128)S(1)} custom-call(f32[128,128]{1,0:T(8,128)S(1)} %cholesky.626), custom_call_target="Cholesky" | custom-call | tf_op jit(solution)/shard_map/jit(cholesky)/cholesky | solution.py:57
  817.3 9.8 custom-call.95
  828.9 12.1 %cholesky.571 = f32[128,128]{1,0:T(8,128)S(1)} custom-call(f32[128,128]{1,0:T(8,128)S(1)} %cholesky.631), custom_call_target="Cholesky" | custom-call | tf_op jit(solution)/shard_map/jit(cholesky)/cholesky | solution.py:57
  841.0 9.8 custom-call.96
  852.3 8.8 cholesky.592
  872.0 18.3 %while.2 = (s32[]{:T(128)}, f32[864,864]{1,0:T(8,128)}, s32[6,2]{0,1:T(2,128)S(1)}, f32[6,128,128]{2,1,0:T(8,128)S(1)}, s32[]{:T(128)}) while((s32[]{:T(128)}, f32[864,864]{1,0:T(8,128)}, s32[6,2]{0,1:T(2,128)S(1)}, f32[6,128,128]{2,1,0:T(8,128)S(1)}, s32[]{:T(128)}) %tuple.129), condition=%wide.while_cond.1, body=%wide.while_body.1.sunk | while | flops 2 | bytes 131189 | solution.py:58
  892.2 69.7 %custom-call.97 = f32[7,128,128]{1,2,0:T(8,128)S(1)} custom-call(f32[7,128,128]{2,1,0:T(8,128)} %pad_maximum_fusion), custom_call_target="InvertDiagBlocksLowerTriangular" | custom-call | tf_op jit(solution)/shard_map/jit(_cho_solve)/triangular_solve | solution.py:58
  (386 shorter events, 452.2 us)
Async XLA Ops:
  7.2 394.5 %all-reduce.18.cloned.1.call-start = ((), (), s32[]{:S(2)}) async-start(), calls=%async_computation.2 | async-start | bytes 245760 | tf_op jit(solution)/shard_map/psum | solution.py:114
  239.5 10.6 %copy-start.8 = (bf16[1,4,8,32,32]{4,3,2,1,0:T(8,128)(2,1)S(1)}, bf16[1,4,8,32,32]{4,3,2,1,0:T(8,128)(2,1)}, u32[]{:S(2)}) copy-start(bf16[1,4,8,32,32]{4,3,2,1,0:T(8,128)(2,1)} %param.6) | copy-start | bytes 196612
  239.6 13.7 %copy-start.10 = (bf16[1,64,128]{2,1,0:T(8,128)(2,1)S(1)}, bf16[1,64,128]{2,1,0:T(8,128)(2,1)}, u32[]{:S(2)}) copy-start(bf16[1,64,128]{2,1,0:T(8,128)(2,1)} %param.7) | copy-start | bytes 49156
  239.6 14.5 %copy-start.15 = (bf16[32,4,3,3,3]{0,1,4,3,2:T(4,128)(2,1)S(1)}, bf16[32,4,3,3,3]{0,1,4,3,2:T(4,128)(2,1)}, u32[]{:S(2)}) copy-start(bf16[32,4,3,3,3]{0,1,4,3,2:T(4,128)(2,1)} %param.8) | copy-start | bytes 20740
  248.9 111.6 %collective-permute-start.2 = (bf16[32,16,16]{0,2,1:T(8,128)(2,1)}, bf16[32,16,16]{0,2,1:T(8,128)(2,1)}, u32[]{:S(2)}, u32[]{:S(2)}) collective-permute-start(bf16[32,16,16]{0,2,1:T(8,128)(2,1)} %fusion.66), channel_id=1, source_target_pairs={{1,0},{2,1},{3,2},{5,4},{6,5},{7,6},{9,8},{10,9},{11,10},{13,12},{... | collective-permute-start | bytes 49160 | tf_op jit(solution)/shard_map/ppermute | solution.py:13
  250.2 3.9 collective-permute-start
  361.6 20.6 %copy-start.4 = (bf16[32,1024]{1,0:T(8,128)(2,1)}, bf16[32,1024]{1,0:T(8,128)(2,1)S(1)}, u32[]{:S(2)}) copy-start(bf16[32,1024]{1,0:T(8,128)(2,1)S(1)} %get-tuple-element.73) | copy-start | bytes 196612
  361.8 6.2 collective-permute-start.1
  368.0 108.3 %all-reduce.14.cloned.1.call-start = ((), (), s32[]{:S(2)}) async-start(), calls=%async_computation | async-start | bytes 245760 | tf_op jit(solution)/shard_map/psum | solution.py:114
  401.6 148.6 %all-reduce.20.cloned.1.call-start = ((), (), s32[]{:S(2)}) async-start(), calls=%async_computation.3 | async-start | bytes 6651904 | tf_op jit(solution)/shard_map/psum | solution.py:114
  402.6 285.1 %all-reduce.16.cloned.1.call-start = ((), (), s32[]{:S(2)}) async-start(), calls=%async_computation.1 | async-start | bytes 6651904 | tf_op jit(solution)/shard_map/psum | solution.py:114
  476.3 74.0 %copy-start.9 = (f32[108,108]{1,0:T(8,128)S(1)}, f32[108,108]{1,0:T(8,128)}, u32[]{:S(2)}) copy-start(f32[108,108]{1,0:T(8,128)} %get-tuple-element.32) | copy-start | bytes 139972
  476.3 93.6 %copy-start.13 = (f32[32,32]{1,0:T(8,128)S(1)}, f32[32,32]{1,0:T(8,128)}, u32[]{:S(2)}) copy-start(f32[32,32]{1,0:T(8,128)} %get-tuple-element.34) | copy-start | bytes 12292
  476.3 100.3 %copy-start.11 = (f32[64,64]{1,0:T(8,128)S(1)}, f32[64,64]{1,0:T(8,128)}, u32[]{:S(2)}) copy-start(f32[64,64]{1,0:T(8,128)} %get-tuple-element.35) | copy-start | bytes 49156
  476.3 113.2 %copy-start.14 = (f32[32,108]{1,0:T(8,128)S(1)}, f32[32,108]{1,0:T(8,128)}, u32[]{:S(2)}) copy-start(f32[32,108]{1,0:T(8,128)} %get-tuple-element.33) | copy-start | bytes 41476
  691.5 4.8 copy-start
  698.6 1.6 copy-start.3
  700.2 12.0 %copy-start.5 = (f32[64,864]{1,0:T(8,128)S(1)}, f32[64,864]{1,0:T(8,128)}, u32[]{:S(2)}) copy-start(f32[64,864]{1,0:T(8,128)} %get-tuple-element.37) | copy-start | bytes 663556
  870.1 0.9 copy-start.16
  870.1 1.9 copy-start.7
  870.4 1.7 copy-start.1
  890.3 78.3 %copy-start.2 = (f32[864,864]{1,0:T(8,128)S(1)}, f32[864,864]{1,0:T(8,128)}, u32[]{:S(2)}) copy-start(f32[864,864]{1,0:T(8,128)} %get-tuple-element.232) | copy-start | bytes 8957956
  967.1 8.2 copy-start.12
  968.6 7.1 copy-start.6
Sparse Core Ops, SparseCore 0:
  368.1 33.4 all-reduce.17
  405.3 70.9 all-reduce.13
  478.7 71.4 all-reduce.19
  553.8 133.8 all-reduce.15
